TPU v7x, 32 devices: a whole 2x2x4 slice. The times are simulated.
32 devices in a mesh: section: 2 (over x), dp: 4 (over z), tensor: 4 (over y, core).
Axes of the slice: x: 2, y: 2, z: 4, core: 2. Of those that a mesh axis runs over, the one named last changes fastest.
Arguments:
- layer_input: bfloat16 [1024, 1024], P('dp'), may hold values from -6 to 6
- output_cotangent: bfloat16 [1024, 1024], P('dp'), may hold values from -6 to 6
- positions: int32 [1024], P('dp'), may hold values from 0 to 255, as said below
- norm_first: float32 [2, 1024], P('section'), may hold values from 0.5 to 1.5
- query_weight: bfloat16 [2, 1024, 512], P('section', None, 'tensor'), may hold values from -0.1875 to 0.1875
- key_projection_weight: bfloat16 [2, 1024, 128], P('section'), may hold values from -0.1875 to 0.1875
- value_projection_weight: bfloat16 [2, 1024, 128], P('section'), may hold values from -0.1875 to 0.1875
- output_weight: bfloat16 [2, 512, 1024], P('section', 'tensor'), may hold values from -1 to 1
- mixer_gate: bfloat16 [2, 1024, 1536], P('section', None, 'tensor'), may hold values from -0.1875 to 0.1875
- mixer_input: bfloat16 [2, 1024, 1536], P('section', None, 'tensor'), may hold values from -0.1875 to 0.1875
- state_input: bfloat16 [2, 1024, 128], P('section'), may hold values from -0.0625 to 0.0625
- state_output: bfloat16 [2, 1024, 128], P('section'), may hold values from -0.0625 to 0.0625
- step_weight: bfloat16 [2, 1024, 24], P('section', None, 'tensor'), may hold values from -0.09375 to 0.09375
- step_bias: float32 [2, 24], P('section', 'tensor'), may hold values from -4 to -1
- decay_log: float32 [2, 24], P('section', 'tensor'), may hold values from -3 to 1
- skip_scale: float32 [2, 24], P('section', 'tensor'), may hold values from 0.5 to 1.5
- mixer_output: bfloat16 [2, 1536, 1024], P('section', 'tensor'), may hold values from -0.15625 to 0.15625
- norm_second: float32 [2, 1024], P('section'), may hold values from 0.5 to 1.5
- hidden_gate: bfloat16 [2, 1024, 2048], P('section', None, 'tensor'), may hold values from -0.1875 to 0.1875
- hidden_up: bfloat16 [2, 1024, 2048], P('section', None, 'tensor'), may hold values from -0.1875 to 0.1875
- hidden_down: bfloat16 [2, 2048, 1024], P('section', 'tensor'), may hold values from -0.125 to 0.125
Outputs:
- block_output: bfloat16 [2, 1024, 1024], P('section', 'dp')
- input_gradient: bfloat16 [2, 1024, 1024], P('section', 'dp')
- grad_norm_first: float32 [2, 1024], P('section')
- grad_query_weight: float32 [2, 1024, 512], P('section', None, 'tensor')
- grad_key_weight: float32 [2, 1024, 128], P('section')
- grad_value_weight: float32 [2, 1024, 128], P('section')
- grad_output_weight: float32 [2, 512, 1024], P('section', 'tensor')
- grad_mixer_gate: float32 [2, 1024, 1536], P('section', None, 'tensor')
- grad_mixer_input: float32 [2, 1024, 1536], P('section', None, 'tensor')
- grad_state_input: float32 [2, 1024, 128], P('section')
- grad_state_output: float32 [2, 1024, 128], P('section')
- grad_step_weight: float32 [2, 1024, 24], P('section', None, 'tensor')
- grad_step_bias: float32 [2, 24], P('section', 'tensor')
- grad_decay_log: float32 [2, 24], P('section', 'tensor')
- grad_skip_scale: float32 [2, 24], P('section', 'tensor')
- grad_mixer_output: float32 [2, 1536, 1024], P('section', 'tensor')
- grad_norm_second: float32 [2, 1024], P('section')
- grad_hidden_gate: float32 [2, 1024, 2048], P('section', None, 'tensor')
- grad_hidden_up: float32 [2, 1024, 2048], P('section', None, 'tensor')
- grad_hidden_down: float32 [2, 2048, 1024], P('section', 'tensor')
Inputs may be any that keep to these rules, and one draw needn't show every extreme that they name: positions count from 0 at a document's first token and rise by one a token; each aligned run of 256 tokens is one sequence whose first token starts a document.
All inputs are finite; a program needn't handle non-finite values.
Results may differ from a plain program's by a relative error of at most 0.035.
Values may be sent and summed in bfloat16 or wider, within the bound.
A program may use at most 128 MiB of HBM per device.

v0:
```python
import jax
import jax.numpy as jnp
from jax import lax
from jax.sharding import PartitionSpec as P

QUERY_HEADS = 8
KEY_VALUE_HEADS = 2
HEAD_DIM = 64
LEN = 256


EPS = 1e-06
highest = lax.Precision.HIGHEST


def shifted(value, axis, steps):
    count = lax.axis_size(axis)
    initial, last = (max(0, -steps), min(count, count - steps))
    return lax.ppermute(value, axis, [(source, source + steps) for source in range(initial, last)])


def rms_scale(layer_token_rows, gain):
    return (
        layer_token_rows
        * lax.rsqrt(jnp.mean(layer_token_rows * layer_token_rows, axis=-1, keepdims=True) + EPS)
        * gain
    )


def visible(positions):
    token_index = jnp.arange(positions.shape[0], dtype=jnp.int32)
    return (token_index[None, :] <= token_index[:, None]) & (
        token_index[None, :] >= token_index[:, None] - positions[:, None]
    )


def silu_product(gate_pre, upper_part):
    return jax.nn.silu(gate_pre) * upper_part


def mixer_core(
    mixer_in,
    gate_z,
    state_in,
    state_out,
    step_raw,
    step_bias,
    decay_log,
    skip_scale,
    causal_visible_mask,
):
    length = mixer_in.shape[0]
    head_count = step_bias.shape[0]
    head_width = mixer_in.shape[1] // head_count
    step_size = jax.nn.softplus(step_raw + step_bias)
    log_decay = jnp.cumsum(step_size * -jnp.exp(decay_log), axis=0).T
    spread = log_decay[:, :, None] - log_decay[:, None, :]
    wide_mask = causal_visible_mask[None]
    decay_factor = jnp.where(wide_mask, jnp.exp(jnp.where(wide_mask, spread, 0.0)), 0.0)
    state_inner = jnp.dot(state_out, state_in.T, precision=highest)
    mixing = state_inner[None] * decay_factor * step_size.T[:, None, :]
    by_head = mixer_in.reshape(length, head_count, head_width).transpose(1, 0, 2)
    mixed_rows = (
        jnp.einsum("hts,hsp->htp", mixing, by_head, precision=highest)
        + skip_scale[:, None, None] * by_head
    )
    return mixed_rows.transpose(1, 0, 2).reshape(length, head_count * head_width) * jax.nn.silu(
        gate_z
    )


def heads_first(layer_token_rows, head_width):
    return layer_token_rows.reshape(
        layer_token_rows.shape[0], layer_token_rows.shape[1] // head_width, head_width
    ).transpose(1, 0, 2)


def rows_first(by_head):
    return by_head.transpose(1, 0, 2).reshape(by_head.shape[1], by_head.shape[0] * by_head.shape[2])


def stacked_heads(layer_token_rows):
    return heads_first(layer_token_rows, HEAD_DIM).reshape(-1, HEAD_DIM)


def unstack_heads(stacked_rows, query_group_width):
    return rows_first(stacked_rows.reshape(query_group_width, -1, HEAD_DIM))


def attention_scores(query_matrix, key_matrix_rows, causal_visible_mask, query_group_width):
    by_query = stacked_heads(query_matrix)
    scores = jnp.dot(
        by_query, key_matrix_rows.T, preferred_element_type=jnp.float32
    ) * HEAD_DIM ** (-0.5)
    wide_mask = jnp.tile(causal_visible_mask, (query_group_width, 1))
    return (jnp.where(wide_mask, scores, -1e30), by_query)


def attention_forward(
    query_matrix, key_matrix_rows, value_matrix_rows, causal_visible_mask, query_group_width
):
    scores, by_query = attention_scores(
        query_matrix, key_matrix_rows, causal_visible_mask, query_group_width
    )
    row_top = jnp.max(scores, axis=-1, keepdims=True)
    logarithm_total = row_top + jnp.log(jnp.sum(jnp.exp(scores - row_top), axis=-1, keepdims=True))
    soft_weights = jnp.exp(scores - logarithm_total).astype(jnp.bfloat16)
    context = jnp.dot(soft_weights, value_matrix_rows, preferred_element_type=jnp.float32)
    return (unstack_heads(context, query_group_width).astype(jnp.bfloat16), logarithm_total)


def attention_reverse_pass(
    query_matrix,
    key_matrix_rows,
    value_matrix_rows,
    logarithm_total,
    context_gradient,
    causal_visible_mask,
    query_group_width,
):
    scores, by_query = attention_scores(
        query_matrix, key_matrix_rows, causal_visible_mask, query_group_width
    )
    probabilities = jnp.exp(scores - logarithm_total)
    by_grad = stacked_heads(context_gradient)
    prob_grad = jnp.dot(by_grad, value_matrix_rows.T, preferred_element_type=jnp.float32)
    row_delta = jnp.sum(probabilities * prob_grad, axis=-1, keepdims=True)
    score_grad = (probabilities * (prob_grad - row_delta) * HEAD_DIM ** (-0.5)).astype(jnp.bfloat16)
    query_gradient = jnp.dot(score_grad, key_matrix_rows, preferred_element_type=jnp.float32)
    key_gradient = jnp.dot(score_grad.T, by_query, preferred_element_type=jnp.float32)
    value_gradient = jnp.dot(
        probabilities.astype(jnp.bfloat16).T, by_grad, preferred_element_type=jnp.float32
    )
    return (unstack_heads(query_gradient, query_group_width), key_gradient, value_gradient)


def mixer_saved_values(
    layer_token_rows, parameters, key_cols, value_cols, causal_visible_mask, query_group_width
):
    normed_input = rms_scale(layer_token_rows, parameters[0]).astype(jnp.bfloat16)
    query_matrix = jnp.dot(normed_input, parameters[1], preferred_element_type=jnp.float32).astype(
        jnp.bfloat16
    )
    key_matrix_rows = jnp.dot(normed_input, key_cols, preferred_element_type=jnp.float32).astype(
        jnp.bfloat16
    )
    value_matrix_rows = jnp.dot(
        normed_input, value_cols, preferred_element_type=jnp.float32
    ).astype(jnp.bfloat16)
    context, logarithm_total = attention_forward(
        query_matrix, key_matrix_rows, value_matrix_rows, causal_visible_mask, query_group_width
    )
    mixer_args = tuple(
        (
            jnp.dot(normed_input, parameters[weight_slot], preferred_element_type=jnp.float32)
            for weight_slot in (6, 5, 7, 8, 9)
        )
    )
    gated = mixer_core(
        mixer_args[0],
        mixer_args[1],
        mixer_args[2],
        mixer_args[3],
        mixer_args[4],
        parameters[10],
        parameters[11],
        parameters[12],
        causal_visible_mask,
    )
    mixer_rows = gated.astype(jnp.bfloat16)
    return (
        normed_input,
        query_matrix,
        key_matrix_rows,
        value_matrix_rows,
        context,
        logarithm_total,
        mixer_args,
        mixer_rows,
    )


def ffn_locals(middle, parameters):
    normed = rms_scale(middle, parameters[14]).astype(jnp.bfloat16)
    gate_pre = jnp.dot(normed, parameters[15], preferred_element_type=jnp.float32)
    upper_part = jnp.dot(normed, parameters[16], preferred_element_type=jnp.float32)
    hidden = silu_product(gate_pre, upper_part).astype(jnp.bfloat16)
    return (normed, gate_pre, upper_part, hidden)


def layer_forward(
    layer_low, parameters, key_cols, value_cols, causal_visible_mask, query_group_width
):
    layer_token_rows = layer_low.astype(jnp.float32)
    gradient_parts = mixer_saved_values(
        layer_token_rows, parameters, key_cols, value_cols, causal_visible_mask, query_group_width
    )
    local_mix = jnp.dot(
        gradient_parts[4], parameters[4], preferred_element_type=jnp.float32
    ) + jnp.dot(gradient_parts[7], parameters[13], preferred_element_type=jnp.float32)
    middle = layer_token_rows + lax.psum(local_mix.astype(jnp.bfloat16), "tensor").astype(
        jnp.float32
    )
    normed, gate_pre, upper_part, hidden = ffn_locals(middle, parameters)
    local_ffn = jnp.dot(hidden, parameters[17], preferred_element_type=jnp.float32)
    result = middle + lax.psum(local_ffn.astype(jnp.bfloat16), "tensor").astype(jnp.float32)
    return (result.astype(jnp.bfloat16), middle)


def layer_backward(
    layer_low,
    middle,
    parameters,
    key_cols,
    value_cols,
    key_value_head,
    causal_visible_mask,
    query_group_width,
    out_grad,
):
    layer_token_rows = layer_low.astype(jnp.float32)
    gradient_parts = mixer_saved_values(
        layer_token_rows, parameters, key_cols, value_cols, causal_visible_mask, query_group_width
    )
    (
        normed_input,
        query_matrix,
        key_matrix_rows,
        value_matrix_rows,
        context,
        logarithm_total,
        mixer_args,
        mixer_rows,
    ) = gradient_parts
    normed, gate_pre, upper_part, hidden = ffn_locals(middle, parameters)
    grad_down = jnp.dot(hidden.T, out_grad, preferred_element_type=jnp.float32)
    hidden_grad = jnp.dot(out_grad, parameters[17].T, preferred_element_type=jnp.float32)
    primal_out, silu_back = jax.vjp(silu_product, gate_pre, upper_part)
    gate_grad, upper_grad = silu_back(hidden_grad)
    gate_grad = gate_grad.astype(jnp.bfloat16)
    upper_grad = upper_grad.astype(jnp.bfloat16)
    grad_gate = jnp.dot(normed.T, gate_grad, preferred_element_type=jnp.float32)
    grad_up = jnp.dot(normed.T, upper_grad, preferred_element_type=jnp.float32)
    local_normed = jnp.dot(
        gate_grad, parameters[15].T, preferred_element_type=jnp.float32
    ) + jnp.dot(upper_grad, parameters[16].T, preferred_element_type=jnp.float32)
    normed_grad = lax.psum(local_normed.astype(jnp.bfloat16), "tensor").astype(jnp.float32)
    primal_out, second_back = jax.vjp(rms_scale, middle, parameters[14])
    middle_part, grad_second = second_back(normed_grad)
    middle_grad = out_grad.astype(jnp.float32) + middle_part
    middle_low = middle_grad.astype(jnp.bfloat16)
    grad_output = jnp.dot(context.T, middle_low, preferred_element_type=jnp.float32)
    context_gradient = jnp.dot(
        middle_low, parameters[4].T, preferred_element_type=jnp.float32
    ).astype(jnp.bfloat16)
    grad_mixer_out = jnp.dot(mixer_rows.T, middle_low, preferred_element_type=jnp.float32)
    mixer_grad = jnp.dot(middle_low, parameters[13].T, preferred_element_type=jnp.float32)
    query_gradient, key_gradient, value_gradient = attention_reverse_pass(
        query_matrix,
        key_matrix_rows,
        value_matrix_rows,
        logarithm_total,
        context_gradient,
        causal_visible_mask,
        query_group_width,
    )

    def core_fixed(
        mixer_in, gate_z, state_in, state_out, step_raw, step_bias, decay_log, skip_scale
    ):
        return mixer_core(
            mixer_in,
            gate_z,
            state_in,
            state_out,
            step_raw,
            step_bias,
            decay_log,
            skip_scale,
            causal_visible_mask,
        )

    primal_out, core_back = jax.vjp(
        core_fixed,
        mixer_args[0],
        mixer_args[1],
        mixer_args[2],
        mixer_args[3],
        mixer_args[4],
        parameters[10],
        parameters[11],
        parameters[12],
    )
    core_grads = core_back(mixer_grad)
    low_grads = [
        query_gradient.astype(jnp.bfloat16),
        key_gradient.astype(jnp.bfloat16),
        value_gradient.astype(jnp.bfloat16),
    ]
    low_grads = low_grads + [
        core_grads[slot_number].astype(jnp.bfloat16) for slot_number in range(5)
    ]
    weights_used = (
        parameters[1],
        key_cols,
        value_cols,
        parameters[6],
        parameters[5],
        parameters[7],
        parameters[8],
        parameters[9],
    )
    proj_grads = [
        jnp.dot(normed_input.T, grad_piece, preferred_element_type=jnp.float32)
        for grad_piece in low_grads
    ]
    local_act = jnp.zeros(layer_token_rows.shape, jnp.float32)
    for grad_piece, weight in zip(low_grads, weights_used):
        local_act = local_act + jnp.dot(grad_piece, weight.T, preferred_element_type=jnp.float32)
    act_grad = lax.psum(local_act.astype(jnp.bfloat16), "tensor").astype(jnp.float32)
    primal_out, first_back = jax.vjp(rms_scale, layer_token_rows, parameters[0])
    rows_part, grad_first = first_back(act_grad)
    input_grad = (middle_grad + rows_part).astype(jnp.bfloat16)
    key_full = lax.dynamic_update_slice_in_dim(
        jnp.zeros(parameters[2].shape, jnp.float32),
        proj_grads[1],
        key_value_head * HEAD_DIM,
        axis=1,
    )
    value_full = lax.dynamic_update_slice_in_dim(
        jnp.zeros(parameters[3].shape, jnp.float32),
        proj_grads[2],
        key_value_head * HEAD_DIM,
        axis=1,
    )
    grads = (
        grad_first,
        proj_grads[0],
        key_full,
        value_full,
        grad_output,
        proj_grads[4],
        proj_grads[3],
        proj_grads[5],
        proj_grads[6],
        proj_grads[7],
        core_grads[5],
        core_grads[6],
        core_grads[7],
        grad_mixer_out,
        grad_second,
        grad_gate,
        grad_up,
        grad_down,
    )
    return (input_grad, grads)


def reduce_grads(grads):
    own_sum = (
        lax.psum(grads[0].astype(jnp.bfloat16), "dp").astype(jnp.float32),
        lax.psum(grads[1].astype(jnp.bfloat16), "dp").astype(jnp.float32),
        lax.psum(grads[4].astype(jnp.bfloat16), "dp").astype(jnp.float32),
        lax.psum(grads[5].astype(jnp.bfloat16), "dp").astype(jnp.float32),
        lax.psum(grads[6].astype(jnp.bfloat16), "dp").astype(jnp.float32),
        lax.psum(grads[9].astype(jnp.bfloat16), "dp").astype(jnp.float32),
        lax.psum(grads[10].astype(jnp.bfloat16), "dp").astype(jnp.float32),
        lax.psum(grads[11].astype(jnp.bfloat16), "dp").astype(jnp.float32),
        lax.psum(grads[12].astype(jnp.bfloat16), "dp").astype(jnp.float32),
        lax.psum(grads[13].astype(jnp.bfloat16), "dp").astype(jnp.float32),
        lax.psum(grads[14].astype(jnp.bfloat16), "dp").astype(jnp.float32),
        lax.psum(grads[15].astype(jnp.bfloat16), "dp").astype(jnp.float32),
        lax.psum(grads[16].astype(jnp.bfloat16), "dp").astype(jnp.float32),
        lax.psum(grads[17].astype(jnp.bfloat16), "dp").astype(jnp.float32),
    )
    common = lax.psum((grads[2], grads[3], grads[7], grads[8]), ("dp", "tensor"))
    return (
        own_sum[0],
        own_sum[1],
        common[0],
        common[1],
        own_sum[2],
        own_sum[3],
        own_sum[4],
        common[2],
        common[3],
        own_sum[5],
        own_sum[6],
        own_sum[7],
        own_sum[8],
        own_sum[9],
        own_sum[10],
        own_sum[11],
        own_sum[12],
        own_sum[13],
    )


def keep_slot(store, item, slot_index, is_valid):
    previous = lax.dynamic_index_in_dim(store, slot_index, 0, keepdims=False)
    return lax.dynamic_update_index_in_dim(
        store, jnp.where(is_valid, item, previous), slot_index, 0
    )


def shards(
    layer_input,
    output_cotangent,
    positions,
    norm_first,
    query_weight,
    key_projection_weight,
    value_projection_weight,
    output_weight,
    mixer_gate,
    mixer_input,
    state_input,
    state_output,
    step_weight,
    step_bias,
    decay_log,
    skip_scale,
    mixer_output,
    norm_second,
    hidden_gate,
    hidden_up,
    hidden_down,
):
    parameters = (
        norm_first[0],
        query_weight[0],
        key_projection_weight[0],
        value_projection_weight[0],
        output_weight[0],
        mixer_gate[0],
        mixer_input[0],
        state_input[0],
        state_output[0],
        step_weight[0],
        step_bias[0],
        decay_log[0],
        skip_scale[0],
        mixer_output[0],
        norm_second[0],
        hidden_gate[0],
        hidden_up[0],
        hidden_down[0],
    )
    section_rank = lax.axis_index("section")
    tensor_position = lax.axis_index("tensor")
    query_group_width = query_weight.shape[-1] // HEAD_DIM
    key_value_head = tensor_position * query_group_width // (QUERY_HEADS // KEY_VALUE_HEADS)
    key_cols = lax.dynamic_slice_in_dim(parameters[2], key_value_head * HEAD_DIM, HEAD_DIM, axis=1)
    value_cols = lax.dynamic_slice_in_dim(
        parameters[3], key_value_head * HEAD_DIM, HEAD_DIM, axis=1
    )
    micro_count = layer_input.shape[0] // LEN
    model_width = layer_input.shape[1]
    time_steps = jnp.arange(micro_count + 1, dtype=jnp.int32)

    def forward_step(carry, time_step):
        produced, kept_inputs, kept_middle, kept_outputs = carry
        incoming = shifted(produced, "section", 1)
        batch_index = time_step - section_rank
        is_valid = (batch_index >= 0) & (batch_index < micro_count)
        slot_index = jnp.clip(batch_index, 0, micro_count - 1)
        causal_visible_mask = visible(positions)
        layer_low = jnp.where(section_rank == 0, layer_input, incoming)
        produced, middle = layer_forward(
            layer_low, parameters, key_cols, value_cols, causal_visible_mask, query_group_width
        )
        kept_inputs = keep_slot(kept_inputs, layer_low, slot_index, is_valid)
        kept_middle = keep_slot(kept_middle, middle, slot_index, is_valid)
        kept_outputs = keep_slot(kept_outputs, produced, slot_index, is_valid)
        return ((produced, kept_inputs, kept_middle, kept_outputs), None)

    forward_init = (
        jnp.zeros((LEN, model_width), jnp.bfloat16),
        jnp.zeros((micro_count, LEN, model_width), jnp.bfloat16),
        jnp.zeros((micro_count, LEN, model_width), jnp.float32),
        jnp.zeros((micro_count, LEN, model_width), jnp.bfloat16),
    )
    forward_final, unused_forward = lax.scan(forward_step, forward_init, time_steps)
    kept_inputs, kept_middle, kept_outputs = (forward_final[1], forward_final[2], forward_final[3])

    def backward_step(carry, time_step):
        sent, kept_grads, running = carry
        incoming_grad = shifted(sent, "section", -1)
        batch_index = time_step - 1 + section_rank
        is_valid = (batch_index >= 0) & (batch_index < micro_count)
        slot_index = jnp.clip(batch_index, 0, micro_count - 1)
        causal_visible_mask = visible(positions)
        out_grad = jnp.where(section_rank == 1, output_cotangent, incoming_grad)
        layer_low = lax.dynamic_index_in_dim(kept_inputs, slot_index, 0, keepdims=False)
        middle = lax.dynamic_index_in_dim(kept_middle, slot_index, 0, keepdims=False)
        sent, step_grads = layer_backward(
            layer_low,
            middle,
            parameters,
            key_cols,
            value_cols,
            key_value_head,
            causal_visible_mask,
            query_group_width,
            out_grad,
        )
        kept_grads = keep_slot(kept_grads, sent, slot_index, is_valid)
        step_grads = tuple((jnp.where(is_valid, grad_piece, 0.0) for grad_piece in step_grads))
        running = tuple((sofar + addend for sofar, addend in zip(running, step_grads)))
        return ((sent, kept_grads, running), None)

    backward_init = (
        jnp.zeros((LEN, model_width), jnp.bfloat16),
        jnp.zeros((micro_count, LEN, model_width), jnp.bfloat16),
        tuple((jnp.zeros(weight.shape, jnp.float32) for weight in parameters)),
    )
    backward_final, unused_backward = lax.scan(backward_step, backward_init, time_steps)
    kept_grads, running = (backward_final[1], backward_final[2])
    running = reduce_grads(running)
    return (
        kept_outputs,
        kept_grads,
        running[0][None],
        running[1][None],
        running[2][None],
        running[3][None],
        running[4][None],
        running[5][None],
        running[6][None],
        running[7][None],
        running[8][None],
        running[9][None],
        running[10][None],
        running[11][None],
        running[12][None],
        running[13][None],
        running[14][None],
        running[15][None],
        running[16][None],
        running[17][None],
    )


def solution(mesh):
    placed = (
        P("dp", None),
        P("dp", None),
        P("dp"),
        P("section", None),
        P("section", None, "tensor"),
        P("section", None, None),
        P("section", None, None),
        P("section", "tensor", None),
        P("section", None, "tensor"),
        P("section", None, "tensor"),
        P("section", None, None),
        P("section", None, None),
        P("section", None, "tensor"),
        P("section", "tensor"),
        P("section", "tensor"),
        P("section", "tensor"),
        P("section", "tensor", None),
        P("section", None),
        P("section", None, "tensor"),
        P("section", None, "tensor"),
        P("section", "tensor", None),
    )
    return jax.shard_map(
        shards,
        mesh=mesh,
        in_specs=placed,
        out_specs=(
            P("section", "dp", None),
            P("section", "dp", None),
            P("section", None),
            P("section", None, "tensor"),
            P("section", None, None),
            P("section", None, None),
            P("section", "tensor", None),
            P("section", None, "tensor"),
            P("section", None, "tensor"),
            P("section", None, None),
            P("section", None, None),
            P("section", None, "tensor"),
            P("section", "tensor"),
            P("section", "tensor"),
            P("section", "tensor"),
            P("section", "tensor", None),
            P("section", None),
            P("section", None, "tensor"),
            P("section", None, "tensor"),
            P("section", "tensor", None),
        ),
        check_vma=False,
    )
```

profile of v0, /device:TPU:0, one launch (start us, length us, event | category | flops | bytes accessed | tf_op | source)
XLA Modules:
  0.0 924.9 jit_solution(10756396381348900885)
XLA Ops:
  15.5 229.6 %while.71 = (s32[]{:T(128)}, bf16[256,1024]{1,0:T(8,128)(2,1)}, bf16[1,256,1024]{2,1,0:T(8,128)(2,1)S(1)}, f32[1,256,1024]{2,1,0:T(8,128)S(1)}, bf16[1,256,1024]...) while((s32[]{:T(128)}, bf16[256,1024]{1,0:T(8,128)(2,1)}, ...), condition=%wide.region_9.10_spmd.clone, body=%wide.region_0.9_spmd.clone.sunk | while | flops 2206970112 | bytes 53623152 | solution.py:483
  15.7 4.9 collective-permute-start
  23.5 8.2 collective-permute-done
  44.9 2.8 fusion.508
  49.1 3.1 fusion.509
  52.3 34.7 %all-reduce.14.cloned.1.call-done = bf16[256,1024]{1,0:T(8,128)(2,1)} async-done(((bf16[256,1024]{1,0:T(8,128)(2,1)}), bf16[256,1024]{1,0:T(8,128)(2,1)}) %all-reduce.14.cloned.1.call-update) | async-done | bytes 524304 | tf_op jit(solution)/shard_map/while/body/eval_jaxpr/psum | solution.py:201
  88.7 2.5 fusion.511
  91.2 3.4 convolution_convert_fusion.32
  94.6 33.6 %all-reduce.16.cloned.1.call-done = bf16[256,1024]{1,0:T(8,128)(2,1)} async-done(((bf16[256,1024]{1,0:T(8,128)(2,1)}), bf16[256,1024]{1,0:T(8,128)(2,1)}) %all-reduce.16.cloned.1.call-update) | async-done | bytes 524304 | tf_op jit(solution)/shard_map/while/body/eval_jaxpr/psum | solution.py:206
  132.6 3.4 collective-permute-start
  139.0 7.2 collective-permute-done
  159.3 2.8 fusion.508
  163.6 3.1 fusion.509
  166.7 34.0 %all-reduce.14.cloned.1.call-done = bf16[256,1024]{1,0:T(8,128)(2,1)} async-done(((bf16[256,1024]{1,0:T(8,128)(2,1)}), bf16[256,1024]{1,0:T(8,128)(2,1)}) %all-reduce.14.cloned.1.call-update) | async-done | bytes 524304 | tf_op jit(solution)/shard_map/while/body/eval_jaxpr/psum | solution.py:201
  202.4 2.5 fusion.511
  204.9 3.4 convolution_convert_fusion.32
  208.4 33.7 %all-reduce.16.cloned.1.call-done = bf16[256,1024]{1,0:T(8,128)(2,1)} async-done(((bf16[256,1024]{1,0:T(8,128)(2,1)}), bf16[256,1024]{1,0:T(8,128)(2,1)}) %all-reduce.16.cloned.1.call-update) | async-done | bytes 524304 | tf_op jit(solution)/shard_map/while/body/eval_jaxpr/psum | solution.py:206
  251.5 328.1 %while.72 = (s32[]{:T(128)}, bf16[256,1024]{1,0:T(8,128)(2,1)}, bf16[1,256,1024]{2,1,0:T(8,128)(2,1)}, f32[1024]{0:T(1024)}, f32[1024,128]{1,0:T(8,128)}, /*inde...) while((s32[]{:T(128)}, bf16[256,1024]{1,0:T(8,128)(2,1)}, ...), condition=%wide.region_34.35_spmd.clone, body=%wide.region_13.34_spmd.clone.sunk | while | flops 5874383360 | bytes 177320816 | solution.py:517
  283.5 3.3 fusion.610
  299.7 2.5 fusion.615
  302.3 3.1 select_add_fusion.23
  309.0 27.1 %all-reduce.18.cloned.1.call-done = bf16[256,1024]{1,0:T(8,128)(2,1)} async-done(((bf16[256,1024]{1,0:T(8,128)(2,1)}), bf16[256,1024]{1,0:T(8,128)(2,1)}) %all-reduce.18.cloned.1.call-update) | async-done | bytes 524304 | tf_op jit(solution)/shard_map/while/body/eval_jaxpr/psum | solution.py:247
  346.7 4.2 fusion.619
  356.1 3.0 fusion.623
  359.1 7.6 reduce-window.66
  367.0 2.6 select_add_fusion.19
  388.7 28.9 %all-reduce.20.cloned.1.call-done = bf16[256,1024]{1,0:T(8,128)(2,1)} async-done(((bf16[256,1024]{1,0:T(8,128)(2,1)}), bf16[256,1024]{1,0:T(8,128)(2,1)}) %all-reduce.20.cloned.1.call-update) | async-done | bytes 524304 | tf_op jit(solution)/shard_map/while/body/eval_jaxpr/psum | solution.py:320
  419.3 3.0 fusion.628
  439.0 3.3 fusion.610
  455.2 2.5 fusion.615
  457.8 3.8 select_add_fusion.23
  461.6 3.4 select_add_fusion.22
  465.0 3.4 select_add_fusion.21
  468.4 23.1 %all-reduce.18.cloned.1.call-done = bf16[256,1024]{1,0:T(8,128)(2,1)} async-done(((bf16[256,1024]{1,0:T(8,128)(2,1)}), bf16[256,1024]{1,0:T(8,128)(2,1)}) %all-reduce.18.cloned.1.call-update) | async-done | bytes 524304 | tf_op jit(solution)/shard_map/while/body/eval_jaxpr/psum | solution.py:247
  502.2 4.2 fusion.619
  511.6 3.0 fusion.623
  514.6 7.6 reduce-window.66
  522.5 3.2 select_add_fusion.19
  541.0 3.1 select_add_fusion.17
  544.2 3.2 select_add_fusion.18
  549.7 25.0 %all-reduce.20.cloned.1.call-done = bf16[256,1024]{1,0:T(8,128)(2,1)} async-done(((bf16[256,1024]{1,0:T(8,128)(2,1)}), bf16[256,1024]{1,0:T(8,128)(2,1)}) %all-reduce.20.cloned.1.call-update) | async-done | bytes 524304 | tf_op jit(solution)/shard_map/while/body/eval_jaxpr/psum | solution.py:320
  576.3 3.0 fusion.628
  579.7 2.8 convert_bitcast_fusion.1
  585.9 2.5 convert_bitcast_fusion.4
  591.4 2.7 convert_bitcast_fusion.2
  598.4 26.0 %all-reduce.1 = (bf16[1,1024]{1,0:T(2,128)(2,1)S(1)}, bf16[1,1024,6]{1,0,2:T(2,128)(2,1)S(1)}, bf16[1,6]{1,0:T(2,128)(2,1)S(1)}, bf16[1,6]{1,0:T(2,128)(2,1)S(1)...) all-reduce(bf16[1,1024]{1,0:T(2,128)(2,1)S(1)} %broadcast_in_dim.35, ...), channel_id=1, replica_groups=mesh['section'=2,'dp'=4,'tensor'=4] {'dp'}, use_global_device_ids=true, to_apply=%region_35.36 | all-reduce | flops 8210 | bytes 32840 | tf_op jit(solution)/shard_map/psum | solution.py:361
  627.8 182.3 %all-reduce.12.cloned.1.call-done = (bf16[1,1024,128]{2,1,0:T(8,128)(2,1)}, bf16[1,128,1024]{2,1,0:T(8,128)(2,1)}, bf16[1,1024,384]{2,1,0:T(8,128)(2,1)}, bf16[1...) async-done(((bf16[1,1024,128]{2,1,0:T(8,128)(2,1)}, ...) | async-done | bytes 6029328 | tf_op jit(solution)/shard_map/psum | solution.py:362
  822.6 89.1 %all-reduce.10.cloned.1.call-done = (f32[1,1024,128]{2,1,0:T(8,128)}, f32[1,1024,128]{2,1,0:T(8,128)}, f32[1,1024,128]{2,1,0:T(8,128)}, f32[1,1024,128]{2,1,0:T(8,128)}) async-done(((f32[1,1024,128]{2,1,0:T(8,128)}, f32[1,1024,128]{2,1,0:T(8,128)}, f32[1,1024,128]{2,1,0:T(8,128)}, f32[1,1024,128]{2,1,0:T(8,128)}), (f32[1,1024,128]{2,1,0:T(8,128)}, f32[1,1024,128]{2,1,0:T(8,128)}, f32[1,1024,128]{2,1,0:T(8,128)}, ...) | async-done | bytes 2097168 | tf_op jit(solution)/shard_map/psum | solution.py:376
  (773 shorter events, 220.9 us)
Async XLA Ops:
  15.6 26.1 %copy-start.26 = (bf16[1024,64]{1,0:T(8,128)(2,1)}, bf16[1024,64]{1,0:T(8,128)(2,1)S(1)}, u32[]{:S(2)}) copy-start(bf16[1024,64]{1,0:T(8,128)(2,1)S(1)} %get-tuple-element.2362) | copy-start | bytes 393220 | tf_op jit(solution)/shard_map/while
  15.6 71.4 %all-reduce.14.cloned.1.call-start = ((), (), s32[]{:S(2)}) async-start(), calls=%async_computation.2 | async-start | bytes 1048576 | tf_op jit(solution)/shard_map/while/body/eval_jaxpr/psum | solution.py:201
  15.7 16.0 %collective-permute-start = (bf16[256,1024]{1,0:T(8,128)(2,1)S(1)}, bf16[256,1024]{1,0:T(8,128)(2,1)S(1)}, u32[]{:S(2)}, u32[]{:S(2)}) collective-permute-start(bf16[256,1024]{1,0:T(8,128)(2,1)S(1)} %broadcast_select_fusion.14), channel_id=1, source_target_pairs={{0,16},{1,17},{2,18},{3,19},{4,20},{5,21},{6,22},{7,23},{8,24},{9,... | collective-permute-start | bytes 1572872 | tf_op jit(solution)/shard_map/while/body/eval_jaxpr/ppermute | solution.py:19
  52.2 76.0 %all-reduce.16.cloned.1.call-start = ((), (), s32[]{:S(2)}) async-start(), calls=%async_computation.3 | async-start | bytes 1048576 | tf_op jit(solution)/shard_map/while/body/eval_jaxpr/psum | solution.py:206
  91.2 37.1 %copy-start.15 = (bf16[1,256,1024]{2,1,0:T(8,128)(2,1)S(1)}, bf16[1,256,1024]{2,1,0:T(8,128)(2,1)}, u32[]{:S(2)}) copy-start(bf16[1,256,1024]{2,1,0:T(8,128)(2,1)} %get-tuple-element.2324) | copy-start | bytes 1572868 | tf_op jit(solution)/shard_map/while
  131.4 24.7 %copy-start.26 = (bf16[1024,64]{1,0:T(8,128)(2,1)}, bf16[1024,64]{1,0:T(8,128)(2,1)S(1)}, u32[]{:S(2)}) copy-start(bf16[1024,64]{1,0:T(8,128)(2,1)S(1)} %get-tuple-element.2362) | copy-start | bytes 393220 | tf_op jit(solution)/shard_map/while
  131.4 69.3 %all-reduce.14.cloned.1.call-start = ((), (), s32[]{:S(2)}) async-start(), calls=%async_computation.2 | async-start | bytes 1048576 | tf_op jit(solution)/shard_map/while/body/eval_jaxpr/psum | solution.py:201
  132.6 13.6 %collective-permute-start = (bf16[256,1024]{1,0:T(8,128)(2,1)S(1)}, bf16[256,1024]{1,0:T(8,128)(2,1)S(1)}, u32[]{:S(2)}, u32[]{:S(2)}) collective-permute-start(bf16[256,1024]{1,0:T(8,128)(2,1)S(1)} %broadcast_select_fusion.14), channel_id=1, source_target_pairs={{0,16},{1,17},{2,18},{3,19},{4,20},{5,21},{6,22},{7,23},{8,24},{9,... | collective-permute-start | bytes 1572872 | tf_op jit(solution)/shard_map/while/body/eval_jaxpr/ppermute | solution.py:19
  166.7 75.3 %all-reduce.16.cloned.1.call-start = ((), (), s32[]{:S(2)}) async-start(), calls=%async_computation.3 | async-start | bytes 1048576 | tf_op jit(solution)/shard_map/while/body/eval_jaxpr/psum | solution.py:206
  204.9 37.1 %copy-start.15 = (bf16[1,256,1024]{2,1,0:T(8,128)(2,1)S(1)}, bf16[1,256,1024]{2,1,0:T(8,128)(2,1)}, u32[]{:S(2)}) copy-start(bf16[1,256,1024]{2,1,0:T(8,128)(2,1)} %get-tuple-element.2324) | copy-start | bytes 1572868 | tf_op jit(solution)/shard_map/while
  267.9 9.8 %copy-start.28 = (bf16[1024,64]{1,0:T(8,128)(2,1)}, bf16[1024,64]{1,0:T(8,128)(2,1)S(1)}, u32[]{:S(2)}) copy-start(bf16[1024,64]{1,0:T(8,128)(2,1)S(1)} %get-tuple-element.2528) | copy-start | bytes 393220 | tf_op jit(solution)/shard_map/while
  267.9 9.8 %copy-start.80 = (bf16[1024,6]{0,1:T(8,128)(2,1)}, bf16[1024,6]{0,1:T(8,128)(2,1)S(1)}, u32[]{:S(2)}) copy-start(bf16[1024,6]{0,1:T(8,128)(2,1)S(1)} %get-tuple-element.2534) | copy-start | bytes 36868 | tf_op jit(solution)/shard_map/while
  267.9 68.1 %all-reduce.18.cloned.1.call-start = ((), (), s32[]{:S(2)}) async-start(), calls=%async_computation.4 | async-start | bytes 1048576 | tf_op jit(solution)/shard_map/while/body/eval_jaxpr/psum | solution.py:247
  268.8 25.9 %collective-permute-start.1 = (bf16[256,1024]{1,0:T(8,128)(2,1)}, bf16[256,1024]{1,0:T(8,128)(2,1)S(1)}, u32[]{:S(2)}, u32[]{:S(2)}) collective-permute-start(bf16[256,1024]{1,0:T(8,128)(2,1)} %broadcast_select_fusion.15), channel_id=1, source_target_pairs={{16,0},{17,1},{18,2},{19,3},{20,4},{21,5},{22,6},{23,7},{24,8},{25... | collective-permute-start | bytes 1572872 | tf_op jit(solution)/shard_map/while/body/eval_jaxpr/ppermute | solution.py:19
  272.2 6.6 copy-start.85
  272.2 8.5 copy-start.68
  274.5 8.9 copy-start.119
  276.8 6.7 copy-start.91
  279.4 7.6 copy-start.38
  302.3 115.4 %all-reduce.20.cloned.1.call-start = ((), (), s32[]{:S(2)}) async-start(), calls=%async_computation.5 | async-start | bytes 1048576 | tf_op jit(solution)/shard_map/while/body/eval_jaxpr/psum | solution.py:320
  387.5 31.7 %copy-start.86 = (f32[256]{0:T(256)S(1)}, f32[256]{0:T(256)}, u32[]{:S(2)}) copy-start(f32[256]{0:T(256)} %copy-done.85) | copy-start | bytes 3076 | tf_op jit(solution)/shard_map/while
  387.5 31.7 %copy-start.96 = (f32[1024]{0:T(1024)S(1)}, f32[1024]{0:T(1024)}, u32[]{:S(2)}) copy-start(f32[1024]{0:T(1024)} %get-tuple-element.2440) | copy-start | bytes 12292 | tf_op jit(solution)/shard_map/while
  387.5 31.7 %copy-start.1 = (bf16[256,1024]{1,0:T(8,128)(2,1)S(1)}, bf16[256,1024]{1,0:T(8,128)(2,1)}, u32[]{:S(2)}) copy-start(bf16[256,1024]{1,0:T(8,128)(2,1)} %all-reduce.18.cloned.1.call-done) | copy-start | bytes 1572868 | tf_op jit(solution)/shard_map/while
  387.5 31.7 %copy-start.88 = (f32[256]{0:T(256)S(1)}, f32[256]{0:T(256)}, u32[]{:S(2)}) copy-start(f32[256]{0:T(256)} %copy-done.87) | copy-start | bytes 3076 | tf_op jit(solution)/shard_map/while
  387.5 34.7 %copy-start.94 = (f32[1024]{0:T(1024)}, f32[1024]{0:T(1024)S(1)}, u32[]{:S(2)}) copy-start(f32[1024]{0:T(1024)S(1)} %select_add_fusion.20) | copy-start | bytes 12292 | tf_op jit(solution)/shard_map/while
  387.6 34.7 %copy-start.107 = (f32[6]{0:T(128)}, f32[6]{0:T(128)S(1)}, u32[]{:S(2)}) copy-start(f32[6]{0:T(128)S(1)} %fusion.638) | copy-start | bytes 76 | tf_op jit(solution)/shard_map/while
  387.6 34.6 %copy-start.110 = (f32[6]{0:T(128)}, f32[6]{0:T(128)S(1)}, u32[]{:S(2)}) copy-start(f32[6]{0:T(128)S(1)} %get-tuple-element.2506) | copy-start | bytes 76 | tf_op jit(solution)/shard_map/while
  387.6 34.6 %copy-start.113 = (f32[6]{0:T(128)}, f32[6]{0:T(128)S(1)}, u32[]{:S(2)}) copy-start(f32[6]{0:T(128)S(1)} %get-tuple-element.2505) | copy-start | bytes 76 | tf_op jit(solution)/shard_map/while
  422.3 10.9 %copy-start.28 = (bf16[1024,64]{1,0:T(8,128)(2,1)}, bf16[1024,64]{1,0:T(8,128)(2,1)S(1)}, u32[]{:S(2)}) copy-start(bf16[1024,64]{1,0:T(8,128)(2,1)S(1)} %get-tuple-element.2528) | copy-start | bytes 393220 | tf_op jit(solution)/shard_map/while
  422.4 10.9 %copy-start.80 = (bf16[1024,6]{0,1:T(8,128)(2,1)}, bf16[1024,6]{0,1:T(8,128)(2,1)S(1)}, u32[]{:S(2)}) copy-start(bf16[1024,6]{0,1:T(8,128)(2,1)S(1)} %get-tuple-element.2534) | copy-start | bytes 36868 | tf_op jit(solution)/shard_map/while
  422.4 69.2 %all-reduce.18.cloned.1.call-start = ((), (), s32[]{:S(2)}) async-start(), calls=%async_computation.4 | async-start | bytes 1048576 | tf_op jit(solution)/shard_map/while/body/eval_jaxpr/psum | solution.py:247
  424.3 25.9 %collective-permute-start.1 = (bf16[256,1024]{1,0:T(8,128)(2,1)}, bf16[256,1024]{1,0:T(8,128)(2,1)S(1)}, u32[]{:S(2)}, u32[]{:S(2)}) collective-permute-start(bf16[256,1024]{1,0:T(8,128)(2,1)} %broadcast_select_fusion.15), channel_id=1, source_target_pairs={{16,0},{17,1},{18,2},{19,3},{20,4},{21,5},{22,6},{23,7},{24,8},{25... | collective-permute-start | bytes 1572872 | tf_op jit(solution)/shard_map/while/body/eval_jaxpr/ppermute | solution.py:19
  427.7 6.6 copy-start.85
  427.7 8.5 copy-start.68
  430.0 8.9 copy-start.119
  432.3 6.7 copy-start.91
  434.9 7.6 copy-start.38
  457.8 116.9 %all-reduce.20.cloned.1.call-start = ((), (), s32[]{:S(2)}) async-start(), calls=%async_computation.5 | async-start | bytes 1048576 | tf_op jit(solution)/shard_map/while/body/eval_jaxpr/psum | solution.py:320
  547.4 28.8 %copy-start.86 = (f32[256]{0:T(256)S(1)}, f32[256]{0:T(256)}, u32[]{:S(2)}) copy-start(f32[256]{0:T(256)} %copy-done.85) | copy-start | bytes 3076 | tf_op jit(solution)/shard_map/while
  547.4 28.8 %copy-start.96 = (f32[1024]{0:T(1024)S(1)}, f32[1024]{0:T(1024)}, u32[]{:S(2)}) copy-start(f32[1024]{0:T(1024)} %get-tuple-element.2440) | copy-start | bytes 12292 | tf_op jit(solution)/shard_map/while
  547.4 28.9 %copy-start.1 = (bf16[256,1024]{1,0:T(8,128)(2,1)S(1)}, bf16[256,1024]{1,0:T(8,128)(2,1)}, u32[]{:S(2)}) copy-start(bf16[256,1024]{1,0:T(8,128)(2,1)} %all-reduce.18.cloned.1.call-done) | copy-start | bytes 1572868 | tf_op jit(solution)/shard_map/while
  547.4 28.9 %copy-start.88 = (f32[256]{0:T(256)S(1)}, f32[256]{0:T(256)}, u32[]{:S(2)}) copy-start(f32[256]{0:T(256)} %copy-done.87) | copy-start | bytes 3076 | tf_op jit(solution)/shard_map/while
  547.4 31.9 %copy-start.94 = (f32[1024]{0:T(1024)}, f32[1024]{0:T(1024)S(1)}, u32[]{:S(2)}) copy-start(f32[1024]{0:T(1024)S(1)} %select_add_fusion.20) | copy-start | bytes 12292 | tf_op jit(solution)/shard_map/while
  547.5 31.8 %copy-start.107 = (f32[6]{0:T(128)}, f32[6]{0:T(128)S(1)}, u32[]{:S(2)}) copy-start(f32[6]{0:T(128)S(1)} %fusion.638) | copy-start | bytes 76 | tf_op jit(solution)/shard_map/while
  547.5 31.8 %copy-start.110 = (f32[6]{0:T(128)}, f32[6]{0:T(128)S(1)}, u32[]{:S(2)}) copy-start(f32[6]{0:T(128)S(1)} %get-tuple-element.2506) | copy-start | bytes 76 | tf_op jit(solution)/shard_map/while
  547.5 31.8 %copy-start.113 = (f32[6]{0:T(128)}, f32[6]{0:T(128)S(1)}, u32[]{:S(2)}) copy-start(f32[6]{0:T(128)S(1)} %get-tuple-element.2505) | copy-start | bytes 76 | tf_op jit(solution)/shard_map/while
  579.6 230.5 %all-reduce.12.cloned.1.call-start = ((), (), s32[]{:S(2)}) async-start(), calls=%async_computation.1 | async-start | bytes 12058624 | tf_op jit(solution)/shard_map/psum | solution.py:362
  594.1 317.5 %all-reduce.10.cloned.1.call-start = ((), (), s32[]{:S(2)}) async-start(), calls=%async_computation | async-start | bytes 4194304 | tf_op jit(solution)/shard_map/psum | solution.py:376
  (180 other events, 493.2 us)
Sparse Core Ops, SparseCore 0:
  52.4 34.5 all-reduce.13
  94.8 33.4 all-reduce.15
  166.8 33.8 all-reduce.13
  208.5 33.5 all-reduce.15
  302.4 33.6 all-reduce.17
  384.1 33.4 all-reduce.19
  457.9 33.6 all-reduce.17
  541.2 33.4 all-reduce.19
Sparse Core Ops, SparseCore 1:
  594.2 215.8 all-reduce.11
  814.5 97.1 all-reduce.9
where the time goes:
time: 936 us; the launch traced here: 925 us
  waiting for transfers between devices  527 us (56%)
  matrix products  183 us (20%)
  other arithmetic  99.9 us (11%)
  local copies, waits for them, and re-layouts  39.4 us (4%)
  blocking collectives  26 us (3%)
  loops' own time  21.9 us (2%)
  between operations  16.4 us (2%)
  starting transfers between devices  11.3 us (1%)
    psum x1, waiting for transfers between devices, reduce_grads(): lax.psum(grads[1].astype(jnp.bfloat16), 'dp').astype(jnp.float32)  182 us
    psum x1, waiting for transfers between devices, reduce_grads(): lax.psum((grads[2], grads[3], grads[7], grads[8]), ('dp', 'tensor'))  89.1 us
    psum x2, waiting for transfers between devices, layer_forward(): lax.psum(local_mix.astype(jnp.bfloat16), 'tensor').astype(jnp.float32)  68.6 us
    psum x2, waiting for transfers between devices, layer_forward(): lax.psum(local_ffn.astype(jnp.bfloat16), 'tensor').astype(jnp.float32)  67.3 us
    psum x2, waiting for transfers between devices, layer_backward(): lax.psum(local_act.astype(jnp.bfloat16), 'tensor').astype(jnp.float32)  54 us
    psum x2, waiting for transfers between devices, layer_backward(): lax.psum(local_normed.astype(jnp.bfloat16), 'tensor').astype(jnp.float32)  50.2 us
    dot_general x8, matrix products, mixer_core(): jnp.einsum('hts,hsp->htp', mixing, by_head, precision=highest)  26.7 us
    psum x1, blocking collectives, reduce_grads(): lax.psum(grads[0].astype(jnp.bfloat16), 'dp').astype(jnp.float32)  26 us
  transfers between devices with their start and end apart: 14, of which 12 were waited for; matrix products, arithmetic and copies ran while one was open for 11% of the time, Pallas kernels for 0%

commit v1 on v0

v1 whole, which is shorter than its diff:
```python
import functools

import jax
import jax.numpy as jnp
from jax import lax
from jax.experimental import pallas as pl
from jax.experimental.pallas import tpu as pltpu
from jax.sharding import PartitionSpec as P

QUERY_HEADS = 8
KEY_VALUE_HEADS = 2
HEAD_DIM = 64
LANES = 128
EPS = 1e-06
f32 = jnp.float32
bf16 = jnp.bfloat16
highest = lax.Precision.HIGHEST
VMEM = pltpu.VMEM


def dot(a, b):
    return jnp.dot(a, b, preferred_element_type=f32)


def dot_nt(a, b):
    return lax.dot_general(a, b, (((1,), (1,)), ((), ())), preferred_element_type=f32)


def dot_tn(a, b):
    return lax.dot_general(a, b, (((0,), (0,)), ((), ())), preferred_element_type=f32)


def tensor_sum_kernel(count, x_ref, out_ref, near, half, far, s_sem, r_sem, fs_sem, fr_sem):
    rows = x_ref.shape[0] // 2
    chips = count // 2
    me = lax.axis_index("tensor")
    core = lax.rem(me, 2)
    chip = lax.div(me, 2)
    mate = chip * 2 + (1 - core)
    far_ids = [lax.rem(chip + k, chips) * 2 + core for k in range(1, chips)]
    barrier = pltpu.get_barrier_semaphore()
    for peer in [mate] + far_ids:
        pl.semaphore_signal(
            barrier, inc=1, device_id={"tensor": peer}, device_id_type=pl.DeviceIdType.MESH
        )
    pl.semaphore_wait(barrier, chips)
    own = pl.ds(pl.multiple_of(core * rows, rows), rows)
    other = pl.ds(pl.multiple_of((1 - core) * rows, rows), rows)

    def copy(src, dst, send, recv, peer):
        return pltpu.make_async_remote_copy(
            src_ref=src,
            dst_ref=dst,
            send_sem=send,
            recv_sem=recv,
            device_id={"tensor": peer},
            device_id_type=pl.DeviceIdType.MESH,
        )

    first = copy(x_ref.at[other], near, s_sem.at[0], r_sem.at[0], mate)
    first.start()
    first.wait()
    half[...] = (x_ref[own, :].astype(f32) + near[...].astype(f32)).astype(bf16)
    across = [
        copy(half, far.at[k], fs_sem.at[k], fr_sem.at[k], far_ids[k]) for k in range(chips - 1)
    ]
    for c in across:
        c.start()
    for c in across:
        c.wait()
    total = half[...].astype(f32)
    for k in range(chips - 1):
        total = total + far[k].astype(f32)
    out_ref[own, :] = total.astype(bf16)
    last = copy(out_ref.at[own], out_ref.at[own], s_sem.at[1], r_sem.at[1], mate)
    last.start()
    last.wait()


def tensor_sum(value, slot):
    count = lax.axis_size("tensor")
    value = value.astype(bf16)
    rows, cols = value.shape
    chips = count // 2
    return pl.pallas_call(
        functools.partial(tensor_sum_kernel, count),
        out_shape=jax.ShapeDtypeStruct((rows, cols), bf16),
        in_specs=[pl.BlockSpec(memory_space=VMEM)],
        out_specs=pl.BlockSpec(memory_space=VMEM),
        scratch_shapes=[
            VMEM((rows // 2, cols), bf16),
            VMEM((rows // 2, cols), bf16),
            VMEM((max(chips - 1, 1), rows // 2, cols), bf16),
            pltpu.SemaphoreType.DMA((2,)),
            pltpu.SemaphoreType.DMA((2,)),
            pltpu.SemaphoreType.DMA((max(chips - 1, 1),)),
            pltpu.SemaphoreType.DMA((max(chips - 1, 1),)),
        ],
        compiler_params=pltpu.CompilerParams(collective_id=slot, has_side_effects=True),
    )(value)


class Cols:
    def __init__(self, q, x, ns):
        self.q = q
        self.k = q
        self.v = q + HEAD_DIM
        self.x = q + 2 * HEAD_DIM
        self.z = self.x + x
        self.si = self.z + x
        self.so = self.si + ns
        self.st = self.so + ns
        self.end = self.st + LANES
        self.width = x
        self.ns = ns


def core_setup(pos_ref, proj_ref, small_ref, c):
    t = proj_ref.shape[0]
    row = lax.broadcasted_iota(jnp.int32, (t, t), 0)
    col = lax.broadcasted_iota(jnp.int32, (t, t), 1)
    seen = (col <= row) & (col >= row - pos_ref[...])
    biased = proj_ref[:, c.st : c.end] + small_ref[0:1, :]
    step = jnp.maximum(biased, 0.0) + jnp.log1p(jnp.exp(-jnp.abs(biased)))
    rate = jnp.exp(small_ref[1:2, :])
    lower = (col <= row).astype(f32)
    decay = jnp.dot(lower, -step * rate, preferred_element_type=f32, precision=highest)
    return seen, biased, step, rate, decay, row, col


def core_forward_kernel(c, heads, pos_ref, proj_ref, small_ref, ctx_ref, rows_ref, lse_ref):
    seen, biased, step, rate, decay, row, col = core_setup(pos_ref, proj_ref, small_ref, c)
    t = proj_ref.shape[0]
    k = proj_ref[:, c.k : c.k + HEAD_DIM].astype(bf16)
    v = proj_ref[:, c.v : c.v + HEAD_DIM].astype(bf16)
    lane = lax.broadcasted_iota(jnp.int32, (t, LANES), 1)
    lse = jnp.zeros((t, LANES), f32)
    for h in range(c.q // HEAD_DIM):
        at = slice(h * HEAD_DIM, (h + 1) * HEAD_DIM)
        s = dot_nt(proj_ref[:, at].astype(bf16), k) * HEAD_DIM ** (-0.5)
        s = jnp.where(seen, s, -1e30)
        top = jnp.max(s, axis=-1, keepdims=True)
        e = jnp.exp(s - top)
        total = jnp.sum(e, axis=-1, keepdims=True)
        lse = jnp.where(lane == h, top + jnp.log(total), lse)
        ctx_ref[:, at] = dot((e * (1.0 / total)).astype(bf16), v).astype(bf16)
    lse_ref[...] = lse
    decay_t = decay.T
    step_t = step.T
    inner = dot_nt(
        proj_ref[:, c.so : c.so + c.ns].astype(bf16), proj_ref[:, c.si : c.si + c.ns].astype(bf16)
    )
    inner = jnp.where(seen, inner, 0.0)
    p = c.width // heads
    for h in range(heads):
        at = slice(h * p, (h + 1) * p)
        spread = jnp.where(seen, decay[:, h : h + 1] - decay_t[h : h + 1, :], 0.0)
        mix = inner * jnp.exp(spread) * step_t[h : h + 1, :]
        x = proj_ref[:, c.x + h * p : c.x + (h + 1) * p]
        z = proj_ref[:, c.z + h * p : c.z + (h + 1) * p]
        y = dot(mix.astype(bf16), x.astype(bf16)) + small_ref[2:3, h : h + 1] * x
        rows_ref[:, at] = (y * z * jax.nn.sigmoid(z)).astype(bf16)


def core_backward_kernel(
    c, heads, pos_ref, proj_ref, small_ref, lse_ref, dctx_ref, dmix_ref, grad_ref, part_ref, colg
):
    seen, biased, step, rate, decay, row, col = core_setup(pos_ref, proj_ref, small_ref, c)
    t = proj_ref.shape[0]
    k = proj_ref[:, c.k : c.k + HEAD_DIM].astype(bf16)
    v = proj_ref[:, c.v : c.v + HEAD_DIM].astype(bf16)
    scale = HEAD_DIM ** (-0.5)
    dk = jnp.zeros((t, HEAD_DIM), f32)
    dv = jnp.zeros((t, HEAD_DIM), f32)
    for h in range(c.q // HEAD_DIM):
        at = slice(h * HEAD_DIM, (h + 1) * HEAD_DIM)
        q = proj_ref[:, at].astype(bf16)
        dctx = dctx_ref[:, at]
        s = jnp.where(seen, dot_nt(q, k) * scale, -1e30)
        prob = jnp.exp(s - lse_ref[:, h : h + 1])
        dp = dot_nt(dctx, v)
        delta = jnp.sum(prob * dp, axis=-1, keepdims=True)
        ds = (prob * (dp - delta) * scale).astype(bf16)
        grad_ref[:, at] = dot(ds, k).astype(bf16)
        dk = dk + dot_tn(ds, q)
        dv = dv + dot_tn(prob.astype(bf16), dctx)
    grad_ref[:, c.k : c.k + HEAD_DIM] = dk.astype(bf16)
    grad_ref[:, c.v : c.v + HEAD_DIM] = dv.astype(bf16)

    decay_t = decay.T
    step_t = step.T
    si = proj_ref[:, c.si : c.si + c.ns].astype(bf16)
    so = proj_ref[:, c.so : c.so + c.ns].astype(bf16)
    inner = jnp.where(seen, dot_nt(so, si), 0.0)
    lane = lax.broadcasted_iota(jnp.int32, (t, LANES), 1)
    lane_row = lax.broadcasted_iota(jnp.int32, (1, LANES), 1)
    colg[...] = jnp.zeros_like(colg)
    row_sum = jnp.zeros((t, LANES), f32)
    dskip = jnp.zeros((1, LANES), f32)
    dinner = jnp.zeros((t, t), f32)
    p = c.width // heads
    for h in range(heads):
        at = slice(h * p, (h + 1) * p)
        spread = jnp.where(seen, decay[:, h : h + 1] - decay_t[h : h + 1, :], 0.0)
        factor = jnp.where(seen, jnp.exp(spread), 0.0)
        timed = factor * step_t[h : h + 1, :]
        mix = (inner * timed).astype(bf16)
        x = proj_ref[:, c.x + h * p : c.x + (h + 1) * p]
        z = proj_ref[:, c.z + h * p : c.z + (h + 1) * p]
        skip = small_ref[2:3, h : h + 1]
        xl = x.astype(bf16)
        y = dot(mix, xl) + skip * x
        sig = jax.nn.sigmoid(z)
        dg = dmix_ref[:, at]
        dy = dg * z * sig
        dyl = dy.astype(bf16)
        grad_ref[:, c.z + h * p : c.z + (h + 1) * p] = (
            dg * y * sig * (1.0 + z * (1.0 - sig))
        ).astype(bf16)
        grad_ref[:, c.x + h * p : c.x + (h + 1) * p] = (dot_tn(mix, dyl) + skip * dy).astype(bf16)
        dskip = jnp.where(
            lane_row == h, jnp.sum(jnp.sum(dy * x, axis=0, keepdims=True), axis=1, keepdims=True), dskip
        )
        dm = dot_nt(dyl, xl)
        dinner = dinner + dm * timed
        g = dm * (inner * factor)
        colg[h : h + 1, :] = jnp.sum(g, axis=0, keepdims=True)
        e = g * step_t[h : h + 1, :]
        row_sum = jnp.where(lane == h, jnp.sum(e, axis=1, keepdims=True), row_sum)
    dinner = dinner.astype(bf16)
    grad_ref[:, c.so : c.so + c.ns] = dot(dinner, si).astype(bf16)
    grad_ref[:, c.si : c.si + c.ns] = dot_tn(dinner, so).astype(bf16)
    col_sum = colg[...].T
    ddecay = row_sum - step * col_sum
    upper = (col >= row).astype(f32)
    tail = jnp.dot(upper, ddecay, preferred_element_type=f32, precision=highest)
    dstep = col_sum - rate * tail
    draw = dstep * jax.nn.sigmoid(biased)
    grad_ref[:, c.st : c.end] = draw.astype(bf16)
    part_ref[...] = jnp.zeros_like(part_ref)
    part_ref[0:1, :] = jnp.sum(draw, axis=0, keepdims=True)
    part_ref[1:2, :] = jnp.sum(tail * (-step * rate), axis=0, keepdims=True)
    part_ref[2:3, :] = dskip


def whole_blocks(number):
    return [pl.BlockSpec(memory_space=VMEM)] * number


def core_forward(c, heads, positions, proj, small):
    t = proj.shape[0]
    return pl.pallas_call(
        functools.partial(core_forward_kernel, c, heads),
        out_shape=(
            jax.ShapeDtypeStruct((t, c.q), bf16),
            jax.ShapeDtypeStruct((t, c.width), bf16),
            jax.ShapeDtypeStruct((t, LANES), f32),
        ),
        in_specs=whole_blocks(3),
        out_specs=tuple(whole_blocks(3)),
        cost_estimate=pl.CostEstimate(flops=10**9, bytes_accessed=10**7, transcendentals=10**6),
    )(positions, proj, small)


def core_backward(c, heads, positions, proj, small, lse, dctx, dmix):
    t = proj.shape[0]
    return pl.pallas_call(
        functools.partial(core_backward_kernel, c, heads),
        out_shape=(
            jax.ShapeDtypeStruct((t, c.end), bf16),
            jax.ShapeDtypeStruct((8, LANES), f32),
        ),
        in_specs=whole_blocks(6),
        out_specs=tuple(whole_blocks(2)),
        scratch_shapes=[VMEM((LANES, t), f32)],
        cost_estimate=pl.CostEstimate(
            flops=2 * 10**9, bytes_accessed=2 * 10**7, transcendentals=10**6
        ),
    )(positions, proj, small, lse, dctx, dmix)


def shifted(value, axis, steps):
    count = lax.axis_size(axis)
    initial, last = (max(0, -steps), min(count, count - steps))
    return lax.ppermute(value, axis, [(source, source + steps) for source in range(initial, last)])


def rms(v):
    return v * lax.rsqrt(jnp.mean(v * v, axis=-1, keepdims=True) + EPS)


def rms_back(v, gain, grad):
    inverse = lax.rsqrt(jnp.mean(v * v, axis=-1, keepdims=True) + EPS)
    unit = v * inverse
    scaled = grad * gain
    back = inverse * (scaled - unit * jnp.mean(scaled * unit, axis=-1, keepdims=True))
    return back, jnp.sum(grad * unit, axis=0)


def layer_forward(low, w, c, heads, positions):
    rows = low.astype(f32)
    normed_input = (rms(rows) * w["n1"]).astype(bf16)
    proj = dot(normed_input, w["cat"])
    ctx, mixer_rows, lse = core_forward(c, heads, positions, proj, w["small"])
    local = dot(ctx, w["out"]) + dot(mixer_rows, w["mo"])
    middle = rows + tensor_sum(local, 0).astype(f32)
    normed = (rms(middle) * w["n2"]).astype(bf16)
    gate_pre = dot(normed, w["hg"])
    upper = dot(normed, w["hu"])
    hidden = (jax.nn.silu(gate_pre) * upper).astype(bf16)
    local = dot(hidden, w["hd"])
    result = (middle + tensor_sum(local, 0).astype(f32)).astype(bf16)
    saved = (rows, normed_input, proj, ctx, mixer_rows, lse, middle, normed, gate_pre, upper, hidden)
    return result, saved


def layer_backward(out_grad, saved, w, c, heads, positions, full):
    rows, normed_input, proj, ctx, mixer_rows, lse, middle, normed, gate_pre, upper, hidden = saved
    dhidden = dot_nt(out_grad, w["hd"])
    sig = jax.nn.sigmoid(gate_pre)
    dgate = (dhidden * upper * sig * (1.0 + gate_pre * (1.0 - sig))).astype(bf16)
    dupper = (dhidden * gate_pre * sig).astype(bf16)
    local = dot_nt(dgate, w["hg"]) + dot_nt(dupper, w["hu"])
    normed_grad = tensor_sum(local, 0).astype(f32)
    back, dn2 = rms_back(middle, w["n2"], normed_grad)
    middle_grad = out_grad.astype(f32) + back
    middle_low = middle_grad.astype(bf16)
    dctx = dot_nt(middle_low, w["out"]).astype(bf16)
    dmix = dot_nt(middle_low, w["mo"])
    grads, parts = core_backward(c, heads, positions, proj, w["small"], lse, dctx, dmix)
    local = dot_nt(grads, w["cat"]).astype(bf16)
    shared_sum = None
    if full:
        kv = jnp.where(w["pick"], jnp.tile(grads[:, c.k : c.k + HEAD_DIM], (1, KEY_VALUE_HEADS)), 0)
        vv = jnp.where(w["pick"], jnp.tile(grads[:, c.v : c.v + HEAD_DIM], (1, KEY_VALUE_HEADS)), 0)
        joint = jnp.concatenate([local, kv, vv, grads[:, c.si : c.st]], axis=1)
        joint = tensor_sum(joint, 1)
        act_grad = joint[:, : local.shape[1]].astype(f32)
        shared_sum = joint[:, local.shape[1] :]
    else:
        act_grad = tensor_sum(local, 0).astype(f32)
    back, dn1 = rms_back(rows, w["n1"], act_grad)
    input_grad = (middle_grad + back).astype(bf16)
    return input_grad, (dgate, dupper, middle_low, grads, parts, shared_sum, dn1, dn2)


def gather(value):
    return lax.all_gather(value, "dp", axis=0, tiled=True)


def shards(
    layer_input,
    output_cotangent,
    positions,
    norm_first,
    query_weight,
    key_projection_weight,
    value_projection_weight,
    output_weight,
    mixer_gate,
    mixer_input,
    state_input,
    state_output,
    step_weight,
    step_bias,
    decay_log,
    skip_scale,
    mixer_output,
    norm_second,
    hidden_gate,
    hidden_up,
    hidden_down,
):
    section = lax.axis_index("section")
    tensor_position = lax.axis_index("tensor")
    group = query_weight.shape[-1] // HEAD_DIM
    head = tensor_position * group // (QUERY_HEADS // KEY_VALUE_HEADS)
    heads = step_bias.shape[-1]
    c = Cols(query_weight.shape[-1], mixer_input.shape[-1], state_input.shape[-1])
    key_cols = lax.dynamic_slice_in_dim(key_projection_weight[0], head * HEAD_DIM, HEAD_DIM, axis=1)
    value_cols = lax.dynamic_slice_in_dim(
        value_projection_weight[0], head * HEAD_DIM, HEAD_DIM, axis=1
    )
    pad = LANES - heads
    cat = jnp.concatenate(
        [
            query_weight[0],
            key_cols,
            value_cols,
            mixer_input[0],
            mixer_gate[0],
            state_input[0],
            state_output[0],
            jnp.pad(step_weight[0], ((0, 0), (0, pad))),
        ],
        axis=1,
    )
    small = jnp.pad(
        jnp.concatenate([step_bias, decay_log, skip_scale], axis=0), ((0, 5), (0, pad))
    )
    kv_width = key_projection_weight.shape[-1]
    w = {
        "n1": norm_first[0],
        "n2": norm_second[0],
        "cat": cat,
        "small": small,
        "out": output_weight[0],
        "mo": mixer_output[0],
        "hg": hidden_gate[0],
        "hu": hidden_up[0],
        "hd": hidden_down[0],
        "pick": (jnp.arange(kv_width) // HEAD_DIM == head)[None, :],
    }
    pos = positions[:, None]
    first, unused = layer_forward(layer_input, w, c, heads, pos)
    incoming = shifted(first, "section", 1)
    low = jnp.where(section == 0, layer_input, incoming)
    block_output, saved = layer_forward(low, w, c, heads, pos)
    rows, normed_input, proj, ctx, mixer_rows, lse, middle, normed, gate_pre, upper, hidden = saved
    normed_input_all = gather(normed_input)
    normed_all = gather(normed)
    hidden_all = gather(hidden)
    mixed_all = gather(jnp.concatenate([ctx, mixer_rows], axis=1))

    sent, unused = layer_backward(output_cotangent, saved, w, c, heads, pos, False)
    incoming = shifted(sent, "section", -1)
    last_section = lax.axis_size("section") - 1
    out_grad = jnp.where(section == last_section, output_cotangent, incoming)
    out_grad_all = gather(out_grad)
    input_grad, extra = layer_backward(out_grad, saved, w, c, heads, pos, True)
    dgate, dupper, middle_low, grads, parts, shared_sum, dn1, dn2 = extra
    ffn_all = gather(jnp.concatenate([dgate, dupper], axis=1))
    middle_all = gather(middle_low)
    own = jnp.concatenate([grads[:, : c.q], grads[:, c.x : c.si], grads[:, c.st :]], axis=1)
    own_all = gather(own)
    width = shared_sum.shape[1]
    vectors = jnp.concatenate([dn1, dn2, parts[:3].reshape(-1)]).astype(bf16)
    extra_rows = -(-vectors.shape[0] // (width * 16)) * 16
    vectors = jnp.pad(vectors, (0, extra_rows * width - vectors.shape[0]))
    t = shared_sum.shape[0]
    tail_all = gather(jnp.concatenate([shared_sum, vectors.reshape(extra_rows, width)], axis=0))
    tail_all = tail_all.reshape(-1, t + extra_rows, width)
    shared_all = tail_all[:, :t].reshape(-1, width)
    summed = jnp.sum(tail_all[:, t:].astype(f32), axis=0).reshape(-1)
    d = dn1.shape[0]
    three = summed[2 * d : 2 * d + 3 * LANES].reshape(3, LANES)[:, :heads]

    grad_down = dot_tn(hidden_all, out_grad_all)
    f = dgate.shape[1]
    grad_gate = dot_tn(normed_all, ffn_all[:, :f])
    grad_up = dot_tn(normed_all, ffn_all[:, f:])
    grad_out = dot_tn(mixed_all[:, : c.q], middle_all)
    grad_mo = dot_tn(mixed_all[:, c.q :], middle_all)
    q, x, ns = c.q, c.width, c.ns
    grad_query = dot_tn(normed_input_all, own_all[:, :q])
    grad_mi = dot_tn(normed_input_all, own_all[:, q : q + x])
    grad_mg = dot_tn(normed_input_all, own_all[:, q + x : q + 2 * x])
    grad_step = dot_tn(normed_input_all, own_all[:, q + 2 * x :])[:, :heads]
    kw = kv_width
    grad_key = dot_tn(normed_input_all, shared_all[:, :kw])
    grad_value = dot_tn(normed_input_all, shared_all[:, kw : 2 * kw])
    grad_si = dot_tn(normed_input_all, shared_all[:, 2 * kw : 2 * kw + ns])
    grad_so = dot_tn(normed_input_all, shared_all[:, 2 * kw + ns :])
    return (
        block_output[None],
        input_grad[None],
        summed[None, :d],
        grad_query[None],
        grad_key[None],
        grad_value[None],
        grad_out[None],
        grad_mg[None],
        grad_mi[None],
        grad_si[None],
        grad_so[None],
        grad_step[None],
        three[0:1],
        three[1:2],
        three[2:3],
        grad_mo[None],
        summed[None, d : 2 * d],
        grad_gate[None],
        grad_up[None],
        grad_down[None],
    )


def solution(mesh):
    rows = P("dp", None)
    by_section = P("section", None)
    split_last = P("section", None, "tensor")
    split_first = P("section", "tensor", None)
    copied = P("section", None, None)
    vector = P("section", "tensor")

    def flat(*args):
        outs = list(shards(*args))
        return tuple(outs)

    return jax.shard_map(
        flat,
        mesh=mesh,
        in_specs=(
            rows,
            rows,
            P("dp"),
            by_section,
            split_last,
            copied,
            copied,
            split_first,
            split_last,
            split_last,
            copied,
            copied,
            split_last,
            vector,
            vector,
            vector,
            split_first,
            by_section,
            split_last,
            split_last,
            split_first,
        ),
        out_specs=(
            P("section", "dp", None),
            P("section", "dp", None),
            by_section,
            split_last,
            copied,
            copied,
            split_first,
            split_last,
            split_last,
            copied,
            copied,
            split_last,
            vector,
            vector,
            vector,
            split_first,
            by_section,
            split_last,
            split_last,
            split_first,
        ),
        check_vma=False,
    )
```

time: 936 us -> 624 us (0.67)
  waiting for transfers between devices: 527 us -> 338 us
  Pallas kernels: 0 us -> 132 us
  matrix products: 183 us -> 75.1 us
  other arithmetic: 99.9 us -> 29.6 us
  blocking collectives: 26 us -> 0 us
  loops' own time: 21.9 us -> 0 us
  local copies, waits for them, and re-layouts: 39.4 us -> 20.6 us
    psum x10 -> x0, waiting for transfers between devices: 511 us -> none  [the longest x1 182 us: reduce_grads(): lax.psum(grads[1].astype(jnp.bfloat16), 'dp').astype(jnp.float32)]
    all_gather x0 -> x9, waiting for transfers between devices: none -> 310 us  [gather(): return lax.all_gather(value, 'dp', axis=0, tiled=True)]
    pallas_call x0 -> x12, Pallas kernels: none -> 132 us  [the longest x8 111 us: tensor_sum(): pl.pallas_call(functools.partial(tensor_sum_kernel, count), out_shape=jax...]
    dot_general x123 -> x36, matrix products: 183 us -> 75.1 us  [the longest x13 32.6 us: dot_tn(): lax.dot_general(a, b, (((0,), (0,)), ((), ())), preferred_element_type=f32)]
    broadcast_in_dim x33 -> x1, other arithmetic: 45.9 us -> 2.97 us  [shards(): input_grad[None]]
    psum x1 -> x0, blocking collectives: 26 us -> none  [reduce_grads(): lax.psum(grads[0].astype(jnp.bfloat16), 'dp').astype(jnp.float32)]
    another operation x12 -> x1, other arithmetic: 22.6 us -> 0.01 us
    another operation x2 -> x0, loops' own time: 21.9 us -> none  [the longest x1 20.2 us: shards(): lax.scan(backward_step, backward_init, time_steps)]
  transfers between devices with their start and end apart: 14 -> 11, of which waited for: 12 -> 11; matrix products, arithmetic and copies ran while one was open for 11% -> 7% of each run, Pallas kernels for 0% -> 2%
where the time goes in v1:
time: 624 us; the launch traced here: 617 us
  waiting for transfers between devices  338 us (54%)
  Pallas kernels  132 us (21%)
  matrix products  75.1 us (12%)
  other arithmetic  29.6 us (5%)
  local copies, waits for them, and re-layouts  20.6 us (3%)
  between operations  15.1 us (2%)
  starting transfers between devices  6.36 us (1%)
    all_gather x9, waiting for transfers between devices, gather(): return lax.all_gather(value, 'dp', axis=0, tiled=True)  310 us
    pallas_call x8, Pallas kernels, tensor_sum(): pl.pallas_call(functools.partial(tensor_sum_kernel, count), out_shape=jax...  111 us
    dot_general x13, matrix products, dot_tn(): lax.dot_general(a, b, (((0,), (0,)), ((), ())), preferred_element_type=f32)  32.6 us
    ppermute x2, waiting for transfers between devices, shifted(): lax.ppermute(value, axis, [(source, source + steps) for source in range(i...  25.9 us
    dot_general x11, matrix products, dot(): return jnp.dot(a, b, preferred_element_type=f32)  21.5 us
    dot_general x12, matrix products, dot_nt(): lax.dot_general(a, b, (((1,), (1,)), ((), ())), preferred_element_type=f32)  20.9 us
    pallas_call x2, Pallas kernels, core_backward(): pl.pallas_call(functools.partial(core_backward_kernel, c, heads), out_sha...  12.7 us
  transfers between devices with their start and end apart: 11, of which 11 were waited for; matrix products, arithmetic and copies ran while one was open for 7% of the time, Pallas kernels for 2%

profile of v1, /device:TPU:0, one launch (start us, length us, event | category | flops | bytes accessed | tf_op | source)
XLA Modules:
  0.0 616.7 jit_solution(12756782916701823976)
XLA Ops:
  12.4 5.4 concatenate.25
  17.8 4.0 fusion.66.proj_ref
  22.4 4.3 shard_map.356
  27.9 2.2 fusion.8.x_ref
  30.1 14.3 %shard_map.357 = bf16[256,1024]{1,0:T(8,128)(2,1)} custom-call(bf16[256,1024]{1,0:T(8,128)(2,1)} %fusion.8.x_ref), custom_call_target="tpu_custom_call" | custom-call | tf_op jit(solution)/shard_map/pallas_call | solution.py:85
  47.6 2.9 convolution_convert_fusion.1.x_ref
  50.5 13.5 %shard_map.358 = bf16[256,1024]{1,0:T(8,128)(2,1)} custom-call(bf16[256,1024]{1,0:T(8,128)(2,1)} %convolution_convert_fusion.1.x_ref), custom_call_target="tpu_custom_call" | custom-call | tf_op jit(solution)/shard_map/pallas_call | solution.py:85
  64.0 2.1 add_convert_fusion.1
  66.1 4.5 collective-permute-start
  71.9 9.8 %collective-permute-done = bf16[256,1024]{1,0:T(8,128)(2,1)} collective-permute-done((bf16[256,1024]{1,0:T(8,128)(2,1)}, bf16[256,1024]{1,0:T(8,128)(2,1)}, u32[]{:S(2)}, u32[]{:S(2)}) %collective-permute-start) | collective-permute-done | bytes 524320 | tf_op jit(solution)/shard_map/ppermute | solution.py:285
  82.2 4.1 fusion.106.proj_ref
  86.3 4.3 shard_map.359
  91.7 2.2 fusion.9.x_ref
  93.8 13.3 %shard_map.360 = bf16[256,1024]{1,0:T(8,128)(2,1)} custom-call(bf16[256,1024]{1,0:T(8,128)(2,1)} %fusion.9.x_ref), custom_call_target="tpu_custom_call" | custom-call | tf_op jit(solution)/shard_map/pallas_call | solution.py:85
  114.2 13.2 %shard_map.362 = bf16[256,1024]{1,0:T(8,128)(2,1)} custom-call(bf16[256,1024]{1,0:T(8,128)(2,1)} %fusion.6.x_ref), custom_call_target="tpu_custom_call" | custom-call | tf_op jit(solution)/shard_map/pallas_call | solution.py:85
  132.7 6.3 %shard_map.363 = (bf16[256,1408]{1,0:T(8,128)(2,1)}, f32[8,128]{1,0:T(8,128)}) custom-call(s32[256,1]{1,0:T(8,128)} %copy.44.pos_ref, f32[256,1408]{1,0:T(8,128)} %fusion.106.proj_ref, f32[8,128]{1,0:T(8,128)} %select_maximum_fusion.small_ref, f32[256,128]{1,0:T(8,128)} %get-tuple-element.32.lse_ref, bf16[256,128]{1,0:T(8,128)(2,1)} %convolution_convert_fusion.5.dctx_ref, ...), custom_call_target="tpu_custom_call" | custom-call | flops 2000000000 | bytes 20000000 | tf_op jit(solution)/shard_map/pallas_call | solution.py:267
  139.1 3.9 convolution_convert_fusion.3.x_ref
  142.9 13.2 %shard_map.364 = bf16[256,1024]{1,0:T(8,128)(2,1)} custom-call(bf16[256,1024]{1,0:T(8,128)(2,1)} %convolution_convert_fusion.3.x_ref), custom_call_target="tpu_custom_call" | custom-call | tf_op jit(solution)/shard_map/pallas_call | solution.py:85
  157.7 2.2 fusion.29
  161.2 16.1 %collective-permute-done.1 = bf16[256,1024]{1,0:T(8,128)(2,1)S(1)} collective-permute-done((bf16[256,1024]{1,0:T(8,128)(2,1)}, bf16[256,1024]{1,0:T(8,128)(2,1)S(1)}, u32[]{:S(2)}, u32[]{:S(2)}) %collective-permute-start.1) | collective-permute-done | bytes 524320 | tf_op jit(solution)/shard_map/ppermute | solution.py:285
  177.4 2.7 multiply_convert_fusion.2
  182.8 13.2 %shard_map.365 = bf16[256,1024]{1,0:T(8,128)(2,1)} custom-call(bf16[256,1024]{1,0:T(8,128)(2,1)} %fusion.7.x_ref), custom_call_target="tpu_custom_call" | custom-call | tf_op jit(solution)/shard_map/pallas_call | solution.py:85
  197.7 2.3 fusion.102
  200.0 2.0 convolution_convert_fusion.4.dctx_ref
  202.0 2.2 fusion.59.dmix_ref
  204.3 6.3 %shard_map.366 = (bf16[256,1408]{1,0:T(8,128)(2,1)}, f32[8,128]{1,0:T(8,128)}) custom-call(s32[256,1]{1,0:T(8,128)} %copy.44.pos_ref, f32[256,1408]{1,0:T(8,128)} %fusion.106.proj_ref, f32[8,128]{1,0:T(8,128)} %select_maximum_fusion.small_ref, f32[256,128]{1,0:T(8,128)} %get-tuple-element.32.lse_ref, bf16[256,128]{1,0:T(8,128)(2,1)} %convolution_convert_fusion.4.dctx_ref, ...), custom_call_target="tpu_custom_call" | custom-call | flops 2000000000 | bytes 20000000 | tf_op jit(solution)/shard_map/pallas_call | solution.py:267
  212.5 3.1 convolution_convert_fusion.2
  217.0 16.7 %shard_map.367 = bf16[256,1536]{1,0:T(8,128)(2,1)} custom-call(bf16[256,1536]{1,0:T(8,128)(2,1)} %pad_maximum_fusion.x_ref), custom_call_target="tpu_custom_call" | custom-call | tf_op jit(solution)/shard_map/pallas_call | solution.py:85
  245.0 13.2 %shard_map.361 = bf16[256,1024]{1,0:T(8,128)(2,1)} custom-call(bf16[256,1024]{1,0:T(8,128)(2,1)} %convolution_convert_fusion.x_ref), custom_call_target="tpu_custom_call" | custom-call | tf_op jit(solution)/shard_map/pallas_call | solution.py:85
  258.3 3.0 fusion.68
  261.3 5.5 all-gather.10.cloned.1.call-done
  267.6 2.3 slice.136
  271.6 42.3 %all-gather.12.cloned.1.call-done = bf16[1024,1024]{1,0:T(8,128)(2,1)} async-done(((bf16[256,1024]{1,0:T(8,128)(2,1)}), bf16[1024,1024]{1,0:T(8,128)(2,1)}) %all-gather.12.cloned.1.call-update) | async-done | bytes 2097168 | tf_op jit(solution)/shard_map/all_gather | solution.py:348
  314.0 3.3 convolution_bitcast_fusion.10
  321.9 38.7 %all-gather.14.cloned.1.call-done = bf16[1024,1024]{1,0:T(8,128)(2,1)} async-done(((bf16[256,1024]{1,0:T(8,128)(2,1)}), bf16[1024,1024]{1,0:T(8,128)(2,1)}) %all-gather.14.cloned.1.call-update) | async-done | bytes 2097168 | tf_op jit(solution)/shard_map/all_gather | solution.py:348
  362.6 26.8 %all-gather.16.cloned.1.call-done = bf16[1024,512]{1,0:T(8,128)(2,1)} async-done(((bf16[256,512]{1,0:T(8,128)(2,1)}), bf16[1024,512]{1,0:T(8,128)(2,1)}) %all-gather.16.cloned.1.call-update) | async-done | bytes 1048592 | tf_op jit(solution)/shard_map/all_gather | solution.py:348
  389.4 47.1 %all-gather.18.cloned.1.call-done = bf16[1024,1024]{1,0:T(8,128)(2,1)} async-done(((bf16[256,1024]{1,0:T(8,128)(2,1)}), bf16[1024,1024]{1,0:T(8,128)(2,1)}) %all-gather.18.cloned.1.call-update) | async-done | bytes 2097168 | tf_op jit(solution)/shard_map/all_gather | solution.py:348
  436.5 3.1 convolution_bitcast_fusion.8
  441.6 2.1 convolution_bitcast_fusion.3
  443.8 2.4 convolution_bitcast_fusion.5
  446.2 2.4 convolution_bitcast_fusion.4
  448.6 34.4 %all-gather.20.cloned.1.call-done = bf16[1024,1024]{1,0:T(8,128)(2,1)} async-done(((bf16[256,1024]{1,0:T(8,128)(2,1)}), bf16[1024,1024]{1,0:T(8,128)(2,1)}) %all-gather.20.cloned.1.call-update) | async-done | bytes 2097168 | tf_op jit(solution)/shard_map/all_gather | solution.py:348
  483.0 46.6 %all-gather.22.cloned.1.call-done = bf16[1024,1024]{1,0:T(8,128)(2,1)} async-done(((bf16[256,1024]{1,0:T(8,128)(2,1)}), bf16[1024,1024]{1,0:T(8,128)(2,1)}) %all-gather.22.cloned.1.call-update) | async-done | bytes 2097168 | tf_op jit(solution)/shard_map/all_gather | solution.py:348
  529.6 4.6 convolution_bitcast_fusion.2
  534.2 2.6 convolution_bitcast_fusion.1
  536.8 21.2 %all-gather.24.cloned.1.call-done = bf16[1024,512]{1,0:T(8,128)(2,1)} async-done(((bf16[256,512]{1,0:T(8,128)(2,1)}), bf16[1024,512]{1,0:T(8,128)(2,1)}) %all-gather.24.cloned.1.call-update) | async-done | bytes 1048592 | tf_op jit(solution)/shard_map/all_gather | solution.py:348
  558.0 47.2 %all-gather.26.cloned.1.call-done = bf16[1024,1024]{1,0:T(8,128)(2,1)} async-done(((bf16[256,1024]{1,0:T(8,128)(2,1)}), bf16[1024,1024]{1,0:T(8,128)(2,1)}) %all-gather.26.cloned.1.call-update) | async-done | bytes 2097168 | tf_op jit(solution)/shard_map/all_gather | solution.py:348
  605.2 4.5 convolution_bitcast_fusion
  (179 shorter events, 58.2 us)
Async XLA Ops:
  7.2 40.4 %copy-start = (bf16[1,512,1024]{2,1,0:T(8,128)(2,1)S(1)}, bf16[1,512,1024]{2,1,0:T(8,128)(2,1)}, u32[]{:S(2)}) copy-start(bf16[1,512,1024]{2,1,0:T(8,128)(2,1)} %param.41) | copy-start | bytes 3145732
  7.2 5.2 copy-start.33
  7.2 5.2 copy-start.29
  7.2 259.5 %all-gather.10.cloned.1.call-start = ((), (), s32[]{:S(2)}) async-start(), calls=%async_computation | async-start | bytes 1392640 | tf_op jit(solution)/shard_map/all_gather | solution.py:348
  12.4 5.4 copy-start.3
  12.4 5.4 copy-start.35
  17.8 4.0 copy-start.39
  17.8 4.0 copy-start.40
  17.8 4.0 copy-start.41
  21.8 4.9 copy-start.20
  22.4 5.4 copy-start.4
  27.9 17.8 %copy-start.36 = (f32[1,1024]{1,0:T(1,128)S(1)}, f32[1,1024]{1,0:T(1,128)}, u32[]{:S(2)}) copy-start(f32[1,1024]{1,0:T(1,128)} %param.38) | copy-start | bytes 12292
  44.3 3.3 copy-start.13
  50.5 20.1 %copy-start.14 = (bf16[256,1024]{1,0:T(8,128)(2,1)S(1)}, bf16[256,1024]{1,0:T(8,128)(2,1)}, u32[]{:S(2)}) copy-start(bf16[256,1024]{1,0:T(8,128)(2,1)} %param.22) | copy-start | bytes 1572868
  66.1 15.6 %collective-permute-start = (bf16[256,1024]{1,0:T(8,128)(2,1)}, bf16[256,1024]{1,0:T(8,128)(2,1)}, u32[]{:S(2)}, u32[]{:S(2)}) collective-permute-start(bf16[256,1024]{1,0:T(8,128)(2,1)} %add_convert_fusion.1), channel_id=1, source_target_pairs={{0,16},{1,17},{2,18},{3,19},{4,20},{5,21},{6,22},{7,23},{8,24},{9,... | collective-permute-start | bytes 1572872 | tf_op jit(solution)/shard_map/ppermute | solution.py:285
  82.2 4.1 copy-start.12
  86.3 4.3 copy-start.21
  93.8 15.9 %copy-start.16 = (bf16[1,1024,512]{2,1,0:T(8,128)(2,1)S(1)}, bf16[1,1024,512]{2,1,0:T(8,128)(2,1)}, u32[]{:S(2)}) copy-start(bf16[1,1024,512]{2,1,0:T(8,128)(2,1)} %param.39) | copy-start | bytes 3145732
  109.7 2.7 copy-start.32
  112.9 14.5 %copy-start.2 = (bf16[256,1024]{1,0:T(8,128)(2,1)S(1)}, bf16[256,1024]{1,0:T(8,128)(2,1)}, u32[]{:S(2)}) copy-start(bf16[256,1024]{1,0:T(8,128)(2,1)} %shard_map.360) | copy-start | bytes 1572868
  128.9 2.6 copy-start.5
  159.9 17.4 %collective-permute-start.1 = (bf16[256,1024]{1,0:T(8,128)(2,1)}, bf16[256,1024]{1,0:T(8,128)(2,1)S(1)}, u32[]{:S(2)}, u32[]{:S(2)}) collective-permute-start(bf16[256,1024]{1,0:T(8,128)(2,1)} %fusion.29), channel_id=1, source_target_pairs={{16,0},{17,1},{18,2},{19,3},{20,4},{21,5},{22,6},{23,7},{24,8},{25... | collective-permute-start | bytes 1572872 | tf_op jit(solution)/shard_map/ppermute | solution.py:285
  177.4 20.3 %copy-start.9 = (bf16[256,1024]{1,0:T(8,128)(2,1)}, bf16[256,1024]{1,0:T(8,128)(2,1)S(1)}, u32[]{:S(2)}) copy-start(bf16[256,1024]{1,0:T(8,128)(2,1)S(1)} %broadcast_select_fusion) | copy-start | bytes 1572868
  177.4 2.8 copy-start.17
  180.2 2.7 copy-start.23
  180.2 2.7 copy-start.26
  197.6 4.4 copy-start.6
  216.1 20.2 %copy-start.38 = (f32[8,128]{1,0:T(8,128)S(1)}, f32[8,128]{1,0:T(8,128)}, u32[]{:S(2)}) copy-start(f32[8,128]{1,0:T(8,128)} %get-tuple-element.35) | copy-start | bytes 12292
  217.0 20.9 %copy-start.28 = (bf16[256,1408]{1,0:T(8,128)(2,1)S(1)}, bf16[256,1408]{1,0:T(8,128)(2,1)}, u32[]{:S(2)}) copy-start(bf16[256,1408]{1,0:T(8,128)(2,1)} %get-tuple-element.34) | copy-start | bytes 2162692
  236.2 2.7 copy-start.34
  237.1 76.9 %all-gather.12.cloned.1.call-start = ((), (), s32[]{:S(2)}) async-start(), calls=%async_computation.1 | async-start | bytes 2621440 | tf_op jit(solution)/shard_map/all_gather | solution.py:348
  237.8 4.0 copy-start.24
  237.8 4.0 copy-start.27
  237.9 122.8 %all-gather.14.cloned.1.call-start = ((), (), s32[]{:S(2)}) async-start(), calls=%async_computation.2 | async-start | bytes 2621440 | tf_op jit(solution)/shard_map/all_gather | solution.py:348
  238.8 4.9 copy-start.22
  238.9 150.6 %all-gather.16.cloned.1.call-start = ((), (), s32[]{:S(2)}) async-start(), calls=%async_computation.3 | async-start | bytes 1310720 | tf_op jit(solution)/shard_map/all_gather | solution.py:348
  240.6 195.9 %all-gather.18.cloned.1.call-start = ((), (), s32[]{:S(2)}) async-start(), calls=%async_computation.4 | async-start | bytes 2621440 | tf_op jit(solution)/shard_map/all_gather | solution.py:348
  241.2 241.8 %all-gather.20.cloned.1.call-start = ((), (), s32[]{:S(2)}) async-start(), calls=%async_computation.5 | async-start | bytes 2621440 | tf_op jit(solution)/shard_map/all_gather | solution.py:348
  241.8 287.8 %all-gather.22.cloned.1.call-start = ((), (), s32[]{:S(2)}) async-start(), calls=%async_computation.6 | async-start | bytes 2621440 | tf_op jit(solution)/shard_map/all_gather | solution.py:348
  242.7 15.6 %copy-start.7 = (bf16[256,1024]{1,0:T(8,128)(2,1)S(1)}, bf16[256,1024]{1,0:T(8,128)(2,1)}, u32[]{:S(2)}) copy-start(bf16[256,1024]{1,0:T(8,128)(2,1)} %shard_map.365) | copy-start | bytes 1572868
  242.7 15.6 %copy-start.10 = (bf16[256,1024]{1,0:T(8,128)(2,1)S(1)}, bf16[256,1024]{1,0:T(8,128)(2,1)}, u32[]{:S(2)}) copy-start(bf16[256,1024]{1,0:T(8,128)(2,1)} %copy-done.9) | copy-start | bytes 1572868
  242.7 315.3 %all-gather.24.cloned.1.call-start = ((), (), s32[]{:S(2)}) async-start(), calls=%async_computation.7 | async-start | bytes 1310720 | tf_op jit(solution)/shard_map/all_gather | solution.py:348
  243.5 361.7 %all-gather.26.cloned.1.call-start = ((), (), s32[]{:S(2)}) async-start(), calls=%async_computation.8 | async-start | bytes 2621440 | tf_op jit(solution)/shard_map/all_gather | solution.py:348
  314.0 3.3 copy-start.1
  314.0 3.3 copy-start.15
  436.5 3.1 copy-start.37
  483.0 51.2 %copy-start.42 = (bf16[1024,1024]{1,0:T(8,128)(2,1)S(1)}, bf16[1024,1024]{1,0:T(8,128)(2,1)}, u32[]{:S(2)}) copy-start(bf16[1024,1024]{1,0:T(8,128)(2,1)} %all-gather.20.cloned.1.call-done) | copy-start | bytes 6291460
  529.6 4.6 copy-start.43
  (7 other events, 11.0 us)
Sparse Core Ops, SparseCore 0:
  237.2 29.5 all-gather.9
  268.9 45.0 all-gather.11
  316.1 44.4 all-gather.13
  362.6 26.7 all-gather.15
  391.4 45.0 all-gather.17
  438.5 44.4 all-gather.19
  485.1 44.4 all-gather.21
  531.2 26.7 all-gather.23
  560.2 45.0 all-gather.25
